TPU v7x, 128 devices: a whole 4x4x4 slice. The times are simulated.
128 devices in a mesh: frame: 4 (over x), pix: 32 (over y, z, core).
Axes of the slice: x: 4, y: 4, z: 4, core: 2. Of those that a mesh axis runs over, the one named last changes fastest.
Arguments:
- frames: bfloat16 [128, 4, 512, 512], P('frame', None, 'pix'), may hold values from -26 to 26
- prev_fg: bfloat16 [128, 4, 512, 512], P('frame', None, 'pix'), may hold values from -3 to 3
- depth_valid: int32 [128, 512, 512], P('frame', 'pix'), may hold values 0 or 1
- sketch: float32 [128, 64], replicated, may hold values from -0.5 to 0.5
- tv_weight: float32 [4], replicated, may hold values from 0.1 to 1
Outputs:
- background: bfloat16 [128, 4, 512, 512], P('frame', None, 'pix')
- foreground: bfloat16 [128, 4, 512, 512], P('frame', None, 'pix')
All inputs are finite; a program needn't handle non-finite values. No bound on the sum of `depth_valid` on one device may be relied on, other than what follows from the above.
Results may differ from a plain program's by a relative error of at most 0.012.
The roundings to bfloat16 on the way count: a program that leaves them out, or rounds other values in their place, can miss the bound.
Values may be sent and summed in bfloat16 or wider, within the bound.
A program may use at most 64 MiB of HBM per device.

v0:
```python
import jax
import jax.numpy as jnp
from jax import lax
from jax.sharding import PartitionSpec as P

POWER = 3
NSWEEP = 5
STEP_SIZE = 0.125


def shortened(shard):

    def short(part):
        return part.astype(jnp.bfloat16) if part.dtype == jnp.float32 else part

    return jax.tree.map(short, shard)


def from_behind(value, axis, steps):
    count = lax.axis_size(axis)
    leading, last = (max(0, -steps), min(count, count - steps))
    return lax.ppermute(value, axis, [(source, source + steps) for source in range(leading, last)])


def exact_dot(left, right):
    return jnp.dot(left, right, precision=lax.Precision.HIGHEST)


def mixing_matrix(gram, sketch):
    basis = sketch
    for turn in range(POWER):
        image = exact_dot(gram, basis)
        factor = jnp.linalg.cholesky(exact_dot(basis.T, image))
        basis = lax.linalg.triangular_solve(
            factor, image, left_side=False, lower=True, transpose_a=True
        )
    image = exact_dot(gram, basis)
    factor = jnp.linalg.cholesky(exact_dot(basis.T, image))
    middle = lax.linalg.triangular_solve(
        factor, exact_dot(basis.T, gram), left_side=True, lower=True
    )
    coeffs = lax.linalg.triangular_solve(
        factor, middle, left_side=True, lower=True, transpose_a=True
    )
    return exact_dot(basis, coeffs)


def pair_rows(left, right):
    return lax.dot_general(
        left, right, (((1,), (1,)), ((), ())), preferred_element_type=jnp.float32
    )


def over_frames(weights, pixels):
    return lax.dot_general(
        weights, pixels, (((0,), (0,)), ((), ())), preferred_element_type=jnp.float32
    )


def dual_update(first, second, down, across, step):
    size = jnp.sqrt(down * down + across * across)
    scale = 1.0 + step * size
    return ((first - step * down) / scale, (second - step * across) / scale)


def col_prev(field):
    return jnp.pad(field[:, :, :, :-1], ((0, 0), (0, 0), (0, 0), (1, 0)))


def col_grad(smooth, last_col):
    next_cols = jnp.pad(smooth[:, :, :, 1:], ((0, 0), (0, 0), (0, 0), (0, 1)))
    return jnp.where(last_col, 0.0, next_cols - smooth)


def local(frames, prev_fg, depth_valid, sketch, tv_weight):
    count, chans, rows, cols = frames.shape
    height = rows * lax.axis_size("pix")
    nval = chans * height * cols
    start_frame = lax.axis_index("frame") * count
    chan_ids = lax.broadcasted_iota(jnp.int32, (1, chans, 1, 1), 1)
    depth_ok = depth_valid[:, None, :, :].astype(jnp.float32)
    valid = jnp.where(chan_ids == chans - 1, depth_ok, jnp.float32(1.0))
    resid = ((frames.astype(jnp.float32) - prev_fg.astype(jnp.float32)) * valid).astype(
        jnp.bfloat16
    )
    flat = resid.reshape(count, chans * rows * cols)
    everyone = lax.all_gather(flat, "frame", axis=0, tiled=True)
    block = pair_rows(everyone, flat)
    summed = lax.psum(block, "pix")
    gram = lax.all_gather(summed, "frame", axis=1, tiled=True)
    gram = gram / nval
    mixing = mixing_matrix(gram, sketch)
    mine = lax.dynamic_slice_in_dim(mixing, start_frame, count, 1).astype(jnp.bfloat16)
    back = over_frames(mine, everyone)
    background = back.reshape(count, chans, rows, cols).astype(jnp.bfloat16)
    rounded = lax.optimization_barrier(background).astype(jnp.float32)
    source = (frames.astype(jnp.float32) - rounded) * valid
    lam = tv_weight.reshape(1, chans, 1, 1)
    step = STEP_SIZE / lam
    last_col = lax.broadcasted_iota(jnp.int32, (1, 1, 1, cols), 3) == cols - 1
    row_ids = lax.axis_index("pix") * rows + lax.broadcasted_iota(jnp.int32, (1, 1, rows, 1), 2)
    last_row = row_ids == height - 1

    def divergence(first, second):
        above = from_behind(shortened(first[:, :, -1:, :]), "pix", 1)
        prev_rows = jnp.concatenate([above, first[:, :, :-1, :]], axis=2)
        return first - prev_rows + (second - col_prev(second))

    first = jnp.zeros_like(source)
    second = jnp.zeros_like(source)
    for sweep in range(NSWEEP):
        smooth = source - lam * divergence(first, second)
        below = from_behind(shortened(smooth[:, :, :1, :]), "pix", -1)
        next_rows = jnp.concatenate([smooth[:, :, 1:, :], below], axis=2)
        down = jnp.where(last_row, 0.0, next_rows - smooth)
        across = col_grad(smooth, last_col)
        first, second = dual_update(first, second, down, across, step)
    smooth = source - lam * divergence(first, second)
    return (background, smooth.astype(jnp.bfloat16))


def solution(mesh):
    placed = (
        P("frame", None, "pix", None),
        P("frame", None, "pix", None),
        P("frame", "pix", None),
        P(),
        P(),
    )
    return jax.shard_map(
        local,
        mesh=mesh,
        in_specs=placed,
        out_specs=(P("frame", None, "pix", None), P("frame", None, "pix", None)),
        check_vma=False,
    )
```

profile of v0, /device:TPU:8, one launch (start us, length us, event | category | flops | bytes accessed | tf_op | source)
XLA Modules:
  0.0 442.0 jit_solution(11430136703876754686)
XLA Ops:
  7.3 1.5 convert_element_type.88
  9.7 3.6 fusion
  13.3 1.5 copy.30
  14.9 0.7 convert_element_type.94
  15.5 1.9 collective-permute-start
  17.5 82.8 %all-gather.2.cloned.1.call-done = bf16[128,32768]{1,0:T(8,128)(2,1)} async-done(((bf16[32,32768]{1,0:T(8,128)(2,1)}), bf16[128,32768]{1,0:T(8,128)(2,1)}) %all-gather.2.cloned.1.call-update) | async-done | bytes 8388624 | tf_op jit(solution)/shard_map/all_gather | solution.py:87
  100.3 6.9 %fusion.61 = f32[128,32]{0,1:T(8,128)S(1)} fusion(bf16[128,32768]{1,0:T(8,128)(2,1)} %all-gather.2.cloned.1.call-done, bf16[32,32768]{1,0:T(8,128)(2,1)} %bitcast.91), kind=kOutput, calls=%fused_computation.132 | convolution fusion | flops 268435456 | bytes 10502144 | tf_op jit(solution)/shard_map/dot_general | solution.py:49
  107.2 110.5 %psum.7 = f32[128,32]{0,1:T(8,128)S(1)} all-reduce(f32[128,32]{0,1:T(8,128)S(1)} %fusion.61), channel_id=1, replica_groups=mesh['frame'=4,'pix'=32] {'pix'}, use_global_device_ids=true, to_apply=%region_0.1 | all-reduce | flops 4096 | bytes 32768 | tf_op jit(solution)/shard_map/psum | solution.py:89
  217.7 12.0 %all_gather.7 = f32[128,128]{0,1:T(8,128)S(1)} all-gather(f32[128,32]{0,1:T(8,128)S(1)} %psum.7), channel_id=1, replica_groups=mesh['frame'=4,'pix'=32] {'frame'}, dimensions={1}, use_global_device_ids=true | all-gather | bytes 81920 | tf_op jit(solution)/shard_map/all_gather | solution.py:90
  230.2 5.8 %cholesky.74 = f32[64,64]{1,0:T(8,128)S(1)} custom-call(f32[64,64]{1,0:T(8,128)S(1)} %add_multiply_fusion), custom_call_target="Cholesky" | custom-call | tf_op jit(solution)/shard_map/jit(cholesky)/cholesky | solution.py:33
  236.7 0.7 fusion.32
  237.4 4.9 %custom-call.13 = f32[1,64,64]{1,2,0:T(8,128)S(1)} custom-call(f32[1,64,64]{2,1,0:T(8,128)S(1)} %fusion.32), custom_call_target="InvertDiagBlocksLowerTriangular" | custom-call | tf_op jit(solution)/shard_map/triangular_solve/custom-call.0 | solution.py:34
  243.0 5.8 %cholesky.85 = f32[64,64]{1,0:T(8,128)S(1)} custom-call(f32[64,64]{1,0:T(8,128)S(1)} %fusion.44), custom_call_target="Cholesky" | custom-call | tf_op jit(solution)/shard_map/jit(cholesky)/cholesky | solution.py:33
  250.2 4.9 %custom-call.14 = f32[1,64,64]{1,2,0:T(8,128)S(1)} custom-call(f32[1,64,64]{2,1,0:T(8,128)S(1)} %fusion.33), custom_call_target="InvertDiagBlocksLowerTriangular" | custom-call | tf_op jit(solution)/shard_map/triangular_solve/custom-call.0 | solution.py:34
  255.8 5.8 %cholesky.96 = f32[64,64]{1,0:T(8,128)S(1)} custom-call(f32[64,64]{1,0:T(8,128)S(1)} %fusion.42), custom_call_target="Cholesky" | custom-call | tf_op jit(solution)/shard_map/jit(cholesky)/cholesky | solution.py:33
  263.0 4.9 %custom-call.15 = f32[1,64,64]{1,2,0:T(8,128)S(1)} custom-call(f32[1,64,64]{2,1,0:T(8,128)S(1)} %fusion.34), custom_call_target="InvertDiagBlocksLowerTriangular" | custom-call | tf_op jit(solution)/shard_map/triangular_solve/custom-call.0 | solution.py:34
  268.9 5.8 %cholesky.107 = f32[64,64]{1,0:T(8,128)S(1)} custom-call(f32[64,64]{1,0:T(8,128)S(1)} %fusion.40), custom_call_target="Cholesky" | custom-call | tf_op jit(solution)/shard_map/jit(cholesky)/cholesky | solution.py:38
  276.1 4.9 %custom-call.10 = f32[1,64,64]{1,2,0:T(8,128)S(1)} custom-call(f32[1,64,64]{2,1,0:T(8,128)S(1)} %fusion.35), custom_call_target="InvertDiagBlocksLowerTriangular" | custom-call | tf_op jit(solution)/shard_map/triangular_solve | solution.py:42
  281.7 4.6 %convolution_convert_fusion = bf16[32,32768]{1,0:T(8,128)(2,1)S(1)} fusion(bf16[128,32768]{1,0:T(8,128)(2,1)} %all-gather.2.cloned.1.call-done, bf16[128,128]{0,1:T(8,128)(2,1)S(1)} %fusion.66, s32[]{:T(128)S(6)} %select_n.43), kind=kOutput, calls=%fused_computation | convolution fusion | flops 269484032 | bytes 10493956 | tf_op jit(solution)/shard_map/dot_general | solution.py:55
  286.3 0.7 copy.31
  287.1 3.5 multiply_subtract_fusion
  290.6 1.9 copy-done.5
  292.5 1.9 collective-permute-start.1
  294.4 2.2 copy-done.6
  296.6 1.1 slice.151
  297.8 0.9 slice-done
  298.7 3.6 subtract_divide_fusion.8
  302.4 2.5 collective-permute-start.2
  304.9 0.7 slice.153
  305.6 7.1 %collective-permute-done.2 = bf16[32,4,1,512]{3,0,2,1:T(8,128)(2,1)S(1)} collective-permute-done((bf16[32,4,1,512]{3,0,2,1:T(8,128)(2,1)S(1)}, bf16[32,4,1,512]{3,0,2,1:T(8,128)(2,1)S(1)}, u32[]{:S(2)}, u32[]{:S(2)}) %collective-permute-start.2) | collective-permute-done | bytes 131104 | tf_op jit(solution)/shard_map/ppermute | solution.py:22
  312.8 5.2 %fusion.4 = f32[32,4,16,512]{3,0,2,1:T(8,128)S(1)} fusion(f32[32,4,16,512]{3,0,2,1:T(8,128)S(1)} %get-tuple-element.17, f32[32,4,15,512]{3,0,2,1:T(8,128)S(1)} %slice.153, f32[32,4,1,512]{3,0,2,1:T(8,128)S(1)} %convert_element_type.96, f32[32,4,16,512]{3,0,2,1:T(8,128)S(1)} %get-tuple-element.16, f32[32,4,16,511]{3,0,2,1:T(8,128)S(1)} %bitcast.88, ...), kind=kLoop, calls=%fused_computation.11 | loop fusion | flops 11534336 | bytes 26206228 | tf_op jit(solution)/shard_map/sub | solution.py:112
  318.0 1.9 collective-permute-start.3
  319.9 2.6 slice.155
  322.5 3.1 slice.157
  325.7 5.9 %subtract_divide_fusion.6 = (f32[32,4,16,512]{3,0,2,1:T(8,128)S(1)}, f32[32,4,16,512]{3,0,2,1:T(8,128)S(1)}) fusion(f32[32,4,16,512]{3,0,2,1:T(8,128)S(1)} %get-tuple-element.16, f32[4]{0:T(128)S(1)} %broadcast_divide_fusion, f32[32,4,16,512]{3,0,2,1:T(8,128)S(1)} %fusion.4, f32[32,4,16,511]{3,0,2,1:T(8,128)} %slice.157, ...), kind=kLoop, calls=%fused_computation.49 | loop fusion | flops 16777216 | bytes 29352480 | tf_op jit(solution)/shard_map/div | solution.py:63
  331.6 2.8 collective-permute-start.4
  334.4 0.7 slice.159
  335.1 6.7 %collective-permute-done.4 = bf16[32,4,1,512]{3,0,2,1:T(8,128)(2,1)S(1)} collective-permute-done((bf16[32,4,1,512]{3,0,2,1:T(8,128)(2,1)S(1)}, bf16[32,4,1,512]{3,0,2,1:T(8,128)(2,1)S(1)}, u32[]{:S(2)}, u32[]{:S(2)}) %collective-permute-start.4) | collective-permute-done | bytes 131104 | tf_op jit(solution)/shard_map/ppermute | solution.py:22
  341.8 5.2 %fusion.8 = f32[32,4,16,512]{3,0,2,1:T(8,128)S(1)} fusion(f32[32,4,16,512]{3,0,2,1:T(8,128)S(1)} %get-tuple-element.15, f32[32,4,15,512]{3,0,2,1:T(8,128)S(1)} %slice.159, f32[32,4,1,512]{3,0,2,1:T(8,128)S(1)} %convert_element_type.98, f32[32,4,16,512]{3,0,2,1:T(8,128)S(1)} %get-tuple-element.14, f32[32,4,16,511]{3,0,2,1:T(8,128)S(1)} %bitcast.86, ...), kind=kLoop, calls=%fused_computation.17 | loop fusion | flops 11534336 | bytes 26206228 | tf_op jit(solution)/shard_map/sub | solution.py:112
  347.1 1.9 collective-permute-start.5
  349.0 2.6 slice.161
  351.6 3.1 slice.163
  354.7 5.9 %subtract_divide_fusion.4 = (f32[32,4,16,512]{3,0,2,1:T(8,128)S(1)}, f32[32,4,16,512]{3,0,2,1:T(8,128)S(1)}) fusion(f32[32,4,16,512]{3,0,2,1:T(8,128)S(1)} %get-tuple-element.14, f32[4]{0:T(128)S(1)} %broadcast_divide_fusion, f32[32,4,16,512]{3,0,2,1:T(8,128)S(1)} %fusion.8, f32[32,4,16,511]{3,0,2,1:T(8,128)} %slice.163, ...), kind=kLoop, calls=%fused_computation.45 | loop fusion | flops 16777216 | bytes 29352480 | tf_op jit(solution)/shard_map/div | solution.py:63
  360.6 2.4 collective-permute-start.6
  363.0 0.7 slice.165
  363.8 7.1 %collective-permute-done.6 = bf16[32,4,1,512]{3,0,2,1:T(8,128)(2,1)S(1)} collective-permute-done((bf16[32,4,1,512]{3,0,2,1:T(8,128)(2,1)S(1)}, bf16[32,4,1,512]{3,0,2,1:T(8,128)(2,1)S(1)}, u32[]{:S(2)}, u32[]{:S(2)}) %collective-permute-start.6) | collective-permute-done | bytes 131104 | tf_op jit(solution)/shard_map/ppermute | solution.py:22
  370.9 5.2 %fusion.12 = f32[32,4,16,512]{3,0,2,1:T(8,128)S(1)} fusion(f32[32,4,16,512]{3,0,2,1:T(8,128)S(1)} %get-tuple-element.13, f32[32,4,15,512]{3,0,2,1:T(8,128)S(1)} %slice.165, f32[32,4,1,512]{3,0,2,1:T(8,128)S(1)} %convert_element_type.100, f32[32,4,16,512]{3,0,2,1:T(8,128)S(1)} %get-tuple-element.12, f32[32,4,16,511]{3,0,2,1:T(8,128)S(1)} %bitcast.87, ...), kind=kLoop, calls=%fused_computation.23 | loop fusion | flops 11534336 | bytes 26206228 | tf_op jit(solution)/shard_map/sub | solution.py:112
  376.1 2.1 collective-permute-start.7
  378.2 2.6 slice.167
  380.8 3.1 slice.169
  383.9 5.9 %subtract_divide_fusion.2 = (f32[32,4,16,512]{3,0,2,1:T(8,128)S(1)}, f32[32,4,16,512]{3,0,2,1:T(8,128)S(1)}) fusion(f32[32,4,16,512]{3,0,2,1:T(8,128)S(1)} %get-tuple-element.12, f32[4]{0:T(128)S(1)} %broadcast_divide_fusion, f32[32,4,16,512]{3,0,2,1:T(8,128)S(1)} %fusion.12, f32[32,4,16,511]{3,0,2,1:T(8,128)} %slice.169, ...), kind=kLoop, calls=%fused_computation.41 | loop fusion | flops 16777216 | bytes 29352480 | tf_op jit(solution)/shard_map/div | solution.py:63
  389.8 2.4 collective-permute-start.8
  392.3 0.7 slice.171
  393.0 7.1 %collective-permute-done.8 = bf16[32,4,1,512]{3,0,2,1:T(8,128)(2,1)S(1)} collective-permute-done((bf16[32,4,1,512]{3,0,2,1:T(8,128)(2,1)S(1)}, bf16[32,4,1,512]{3,0,2,1:T(8,128)(2,1)S(1)}, u32[]{:S(2)}, u32[]{:S(2)}) %collective-permute-start.8) | collective-permute-done | bytes 131104 | tf_op jit(solution)/shard_map/ppermute | solution.py:22
  400.1 5.2 %fusion.16 = f32[32,4,16,512]{3,0,2,1:T(8,128)S(1)} fusion(f32[32,4,16,512]{3,0,2,1:T(8,128)S(1)} %get-tuple-element.11, f32[32,4,15,512]{3,0,2,1:T(8,128)S(1)} %slice.171, f32[32,4,1,512]{3,0,2,1:T(8,128)S(1)} %convert_element_type.102, f32[32,4,16,512]{3,0,2,1:T(8,128)S(1)} %get-tuple-element.10, f32[32,4,16,511]{3,0,2,1:T(8,128)S(1)} %bitcast.85, ...), kind=kLoop, calls=%fused_computation.29 | loop fusion | flops 11534336 | bytes 26206228 | tf_op jit(solution)/shard_map/sub | solution.py:112
  405.4 1.9 collective-permute-start.9
  407.3 2.6 slice.173
  409.9 3.1 slice.175
  413.0 5.9 %subtract_divide_fusion = (f32[32,4,16,512]{3,0,2,1:T(8,128)S(1)}, f32[32,4,16,512]{3,0,2,1:T(8,128)S(1)}) fusion(f32[32,4,16,512]{3,0,2,1:T(8,128)S(1)} %get-tuple-element.10, f32[4]{0:T(128)S(1)} %broadcast_divide_fusion, f32[32,4,16,512]{3,0,2,1:T(8,128)S(1)} %fusion.16, f32[32,4,16,511]{3,0,2,1:T(8,128)} %slice.175, ...), kind=kLoop, calls=%fused_computation.37 | loop fusion | flops 16777216 | bytes 29352480 | tf_op jit(solution)/shard_map/div | solution.py:63
  418.9 2.6 collective-permute-start.10
  421.5 0.7 slice.177
  422.3 5.0 %collective-permute-done.10 = bf16[32,4,1,512]{3,0,2,1:T(8,128)(2,1)S(1)} collective-permute-done((bf16[32,4,1,512]{3,0,2,1:T(8,128)(2,1)S(1)}, bf16[32,4,1,512]{3,0,2,1:T(8,128)(2,1)S(1)}, u32[]{:S(2)}, u32[]{:S(2)}) %collective-permute-start.10) | collective-permute-done | bytes 131104 | tf_op jit(solution)/shard_map/ppermute | solution.py:22
  427.3 5.1 %fusion.21 = bf16[32,4,16,512]{3,0,2,1:T(8,128)(2,1)S(1)} fusion(f32[32,4,16,512]{3,0,2,1:T(8,128)S(1)} %get-tuple-element.9, f32[32,4,15,512]{3,0,2,1:T(8,128)S(1)} %slice.177, f32[32,4,1,512]{3,0,2,1:T(8,128)S(1)} %convert_element_type.104, f32[32,4,16,512]{3,0,2,1:T(8,128)S(1)} %get-tuple-element.8, f32[32,4,16,511]{3,0,2,1:T(8,128)S(1)} %bitcast.89, ...), kind=kLoop, calls=%fused_computation.36 | loop fusion | flops 12582912 | bytes 24109076 | tf_op jit(solution)/shard_map/convert_element_type | solution.py:119
  432.5 2.5 copy.29
  (86 shorter events, 9.7 us)
Async XLA Ops:
  7.2 222.6 %copy-start = (f32[128,64]{0,1:T(8,128)S(1)}, f32[128,64]{0,1:T(8,128)}, u32[]{:S(2)}) copy-start(f32[128,64]{0,1:T(8,128)} %param.11) | copy-start | bytes 98308
  7.2 2.2 copy-start.2
  7.2 93.1 %all-gather.2.cloned.1.call-start = ((), (), s32[]{:S(2)}) async-start(), calls=%async_computation | async-start | bytes 10485760 | tf_op jit(solution)/shard_map/all_gather | solution.py:87
  7.2 2.5 copy-start.7
  13.3 4.2 copy-start.8
  15.5 271.5 %collective-permute-start = (bf16[32,4,1,512]{3,0,2,1:T(8,128)(2,1)}, bf16[32,4,1,512]{3,0,2,1:T(8,128)(2,1)S(1)}, u32[]{:S(2)}, u32[]{:S(2)}) collective-permute-start(bf16[32,4,1,512]{3,0,2,1:T(8,128)(2,1)} %convert_element_type.94), channel_id=1, source_target_pairs={{0,1},{1,2},{2,3},{3,4},{4,5},{5,6},{6,7},{7,8},{8,9},{9,10},{10,1... | collective-permute-start | bytes 393224 | tf_op jit(solution)/shard_map/ppermute | solution.py:22
  287.0 3.5 copy-start.3
  290.5 1.9 copy-start.5
  292.5 5.3 %collective-permute-start.1 = (bf16[32,4,1,512]{3,0,2,1:T(8,128)(2,1)S(1)}, bf16[32,4,1,512]{3,0,2,1:T(8,128)(2,1)S(1)}, u32[]{:S(2)}, u32[]{:S(2)}) collective-permute-start(bf16[32,4,1,512]{3,0,2,1:T(8,128)(2,1)S(1)} %slice.198), channel_id=1, source_target_pairs={{1,0},{2,1},{3,2},{4,3},{5,4},{6,5},{7,6},{8,7},{9,8},{10,9},{11,1... | collective-permute-start | bytes 393224 | tf_op jit(solution)/shard_map/ppermute | solution.py:22
  294.4 2.2 copy-start.6
  296.6 2.1 slice-start
  302.4 10.4 %copy-start.4 = (bf16[4,8,64,512]{3,2,1,0:T(8,128)(2,1)S(1)}, bf16[4,8,64,512]{3,2,1,0:T(8,128)(2,1)}, u32[]{:S(2)}) copy-start(bf16[4,8,64,512]{3,2,1,0:T(8,128)(2,1)} %copy-done.3) | copy-start | bytes 6291460
  302.4 10.4 %collective-permute-start.2 = (bf16[32,4,1,512]{3,0,2,1:T(8,128)(2,1)S(1)}, bf16[32,4,1,512]{3,0,2,1:T(8,128)(2,1)S(1)}, u32[]{:S(2)}, u32[]{:S(2)}) collective-permute-start(bf16[32,4,1,512]{3,0,2,1:T(8,128)(2,1)S(1)} %slice.197), channel_id=1, source_target_pairs={{0,1},{1,2},{2,3},{3,4},{4,5},{5,6},{6,7},{7,8},{8,9},{9,10},{10,1... | collective-permute-start | bytes 393224 | tf_op jit(solution)/shard_map/ppermute | solution.py:22
  318.0 7.6 %collective-permute-start.3 = (bf16[32,4,1,512]{3,0,2,1:T(8,128)(2,1)S(1)}, bf16[32,4,1,512]{3,0,2,1:T(8,128)(2,1)S(1)}, u32[]{:S(2)}, u32[]{:S(2)}) collective-permute-start(bf16[32,4,1,512]{3,0,2,1:T(8,128)(2,1)S(1)} %slice.196), channel_id=1, source_target_pairs={{1,0},{2,1},{3,2},{4,3},{5,4},{6,5},{7,6},{8,7},{9,8},{10,9},{11,1... | collective-permute-start | bytes 393224 | tf_op jit(solution)/shard_map/ppermute | solution.py:22
  331.6 10.2 %collective-permute-start.4 = (bf16[32,4,1,512]{3,0,2,1:T(8,128)(2,1)S(1)}, bf16[32,4,1,512]{3,0,2,1:T(8,128)(2,1)S(1)}, u32[]{:S(2)}, u32[]{:S(2)}) collective-permute-start(bf16[32,4,1,512]{3,0,2,1:T(8,128)(2,1)S(1)} %slice.195), channel_id=1, source_target_pairs={{0,1},{1,2},{2,3},{3,4},{4,5},{5,6},{6,7},{7,8},{8,9},{9,10},{10,1... | collective-permute-start | bytes 393224 | tf_op jit(solution)/shard_map/ppermute | solution.py:22
  347.1 7.6 %collective-permute-start.5 = (bf16[32,4,1,512]{3,0,2,1:T(8,128)(2,1)S(1)}, bf16[32,4,1,512]{3,0,2,1:T(8,128)(2,1)S(1)}, u32[]{:S(2)}, u32[]{:S(2)}) collective-permute-start(bf16[32,4,1,512]{3,0,2,1:T(8,128)(2,1)S(1)} %slice.194), channel_id=1, source_target_pairs={{1,0},{2,1},{3,2},{4,3},{5,4},{6,5},{7,6},{8,7},{9,8},{10,9},{11,1... | collective-permute-start | bytes 393224 | tf_op jit(solution)/shard_map/ppermute | solution.py:22
  360.6 10.2 %collective-permute-start.6 = (bf16[32,4,1,512]{3,0,2,1:T(8,128)(2,1)S(1)}, bf16[32,4,1,512]{3,0,2,1:T(8,128)(2,1)S(1)}, u32[]{:S(2)}, u32[]{:S(2)}) collective-permute-start(bf16[32,4,1,512]{3,0,2,1:T(8,128)(2,1)S(1)} %slice.193), channel_id=1, source_target_pairs={{0,1},{1,2},{2,3},{3,4},{4,5},{5,6},{6,7},{7,8},{8,9},{9,10},{10,1... | collective-permute-start | bytes 393224 | tf_op jit(solution)/shard_map/ppermute | solution.py:22
  376.1 7.8 %collective-permute-start.7 = (bf16[32,4,1,512]{3,0,2,1:T(8,128)(2,1)S(1)}, bf16[32,4,1,512]{3,0,2,1:T(8,128)(2,1)S(1)}, u32[]{:S(2)}, u32[]{:S(2)}) collective-permute-start(bf16[32,4,1,512]{3,0,2,1:T(8,128)(2,1)S(1)} %slice.192), channel_id=1, source_target_pairs={{1,0},{2,1},{3,2},{4,3},{5,4},{6,5},{7,6},{8,7},{9,8},{10,9},{11,1... | collective-permute-start | bytes 393224 | tf_op jit(solution)/shard_map/ppermute | solution.py:22
  389.8 10.2 %collective-permute-start.8 = (bf16[32,4,1,512]{3,0,2,1:T(8,128)(2,1)S(1)}, bf16[32,4,1,512]{3,0,2,1:T(8,128)(2,1)S(1)}, u32[]{:S(2)}, u32[]{:S(2)}) collective-permute-start(bf16[32,4,1,512]{3,0,2,1:T(8,128)(2,1)S(1)} %slice.191), channel_id=1, source_target_pairs={{0,1},{1,2},{2,3},{3,4},{4,5},{5,6},{6,7},{7,8},{8,9},{9,10},{10,1... | collective-permute-start | bytes 393224 | tf_op jit(solution)/shard_map/ppermute | solution.py:22
  405.4 7.6 %collective-permute-start.9 = (bf16[32,4,1,512]{3,0,2,1:T(8,128)(2,1)S(1)}, bf16[32,4,1,512]{3,0,2,1:T(8,128)(2,1)S(1)}, u32[]{:S(2)}, u32[]{:S(2)}) collective-permute-start(bf16[32,4,1,512]{3,0,2,1:T(8,128)(2,1)S(1)} %slice.190), channel_id=1, source_target_pairs={{1,0},{2,1},{3,2},{4,3},{5,4},{6,5},{7,6},{8,7},{9,8},{10,9},{11,1... | collective-permute-start | bytes 393224 | tf_op jit(solution)/shard_map/ppermute | solution.py:22
  418.9 8.4 %collective-permute-start.10 = (bf16[32,4,1,512]{3,0,2,1:T(8,128)(2,1)S(1)}, bf16[32,4,1,512]{3,0,2,1:T(8,128)(2,1)S(1)}, u32[]{:S(2)}, u32[]{:S(2)}) collective-permute-start(bf16[32,4,1,512]{3,0,2,1:T(8,128)(2,1)S(1)} %slice.189), channel_id=1, source_target_pairs={{0,1},{1,2},{2,3},{3,4},{4,5},{5,6},{6,7},{7,8},{8,9},{9,10},{10,1... | collective-permute-start | bytes 393224 | tf_op jit(solution)/shard_map/ppermute | solution.py:22
  427.3 7.6 %copy-start.1 = (f32[128,64]{0,1:T(8,128)S(1)}, f32[128,64]{0,1:T(8,128)}, u32[]{:S(2)}) copy-start(f32[128,64]{0,1:T(8,128)} %param.11) | copy-start | bytes 98308
Sparse Core Ops, SparseCore 0:
  15.0 85.3 all-gather.1
where the time goes:
time: 448 us; the launch traced here: 442 us
  blocking collectives  122 us (27%)
  waiting for transfers between devices  116 us (26%)
  other arithmetic  110 us (25%)
  local copies, waits for them, and re-layouts  39.3 us (9%)
  starting transfers between devices  24.5 us (5%)
  between operations  15 us (3%)
  matrix products  14.7 us (3%)
    psum x1, blocking collectives, local(): summed = lax.psum(block, 'pix')  110 us
    all_gather x1, waiting for transfers between devices, local(): everyone = lax.all_gather(flat, 'frame', axis=0, tiled=True)  82.8 us
    ppermute x11, waiting for transfers between devices, from_behind(): lax.ppermute(value, axis, [(source, source + steps) for source in range(l...  33 us
    div x5, other arithmetic, dual_update(): return ((first - step * down) / scale, (second - step * across) / scale)  27.1 us
    another operation x12, other arithmetic, mixing_matrix(): factor = jnp.linalg.cholesky(exact_dot(basis.T, image))  26.1 us
    ppermute x11, starting transfers between devices, from_behind(): lax.ppermute(value, axis, [(source, source + steps) for source in range(l...  24.5 us
    sub x5, other arithmetic, local(): smooth = source - lam * divergence(first, second)  24.3 us
    another operation x6, other arithmetic, mixing_matrix(): lax.linalg.triangular_solve(factor, image, left_side=False, lower=True, t...  16.6 us
  transfers between devices with their start and end apart: 12, of which 6 were waited for; matrix products, arithmetic and copies ran while one was open for 21% of the time, Pallas kernels for 0%

commit v1 on v0

--- a/solution.py
+++ b/solution.py
@@ -86,7 +86,9 @@
     flat = resid.reshape(count, chans * rows * cols)
     everyone = lax.all_gather(flat, "frame", axis=0, tiled=True)
     block = pair_rows(everyone, flat)
-    summed = lax.psum(block, "pix")
+    summed = block
+    for hop in (1, 2, 4, 8, 16):
+        summed = summed + lax.ppermute(summed, "pix", [(dev, dev ^ hop) for dev in range(32)])
     gram = lax.all_gather(summed, "frame", axis=1, tiled=True)
     gram = gram / nval
     mixing = mixing_matrix(gram, sketch)

time: 448 us -> 351 us (0.78)
  blocking collectives: 122 us -> 12.1 us
  starting transfers between devices: 24.5 us -> 31.4 us
  waiting for transfers between devices: 116 us -> 121 us
    psum x1 -> x0, blocking collectives: 110 us -> none  [local(): summed = lax.psum(block, 'pix')]
    ppermute x0 -> x5, waiting for transfers between devices: none -> 10.1 us  [local(): lax.ppermute(summed, 'pix', [(dev, dev ^ hop) for dev in range(32)])]
    ppermute x11, waiting for transfers between devices: 33 us -> 25.7 us  [from_behind(): lax.ppermute(value, axis, [(source, source + steps) for source in range(l...]
    ppermute x0 -> x5, starting transfers between devices: none -> 6.95 us  [local(): lax.ppermute(summed, 'pix', [(dev, dev ^ hop) for dev in range(32)])]
  transfers between devices with their start and end apart: 12 -> 17, of which waited for: 6 -> 10; matrix products, arithmetic and copies ran while one was open for 21% -> 25% of each run, Pallas kernels for 0% -> 0%
where the time goes in v1:
time: 351 us; the launch traced here: 344 us
  waiting for transfers between devices  121 us (34%)
  other arithmetic  110 us (31%)
  local copies, waits for them, and re-layouts  39.5 us (11%)
  starting transfers between devices  31.4 us (9%)
  between operations  15 us (4%)
  matrix products  14.7 us (4%)
  blocking collectives  12.1 us (3%)
    all_gather x1, waiting for transfers between devices, local(): everyone = lax.all_gather(flat, 'frame', axis=0, tiled=True)  85.5 us
    div x5, other arithmetic, dual_update(): return ((first - step * down) / scale, (second - step * across) / scale)  27.1 us
    another operation x12, other arithmetic, mixing_matrix(): factor = jnp.linalg.cholesky(exact_dot(basis.T, image))  26.1 us
    ppermute x11, waiting for transfers between devices, from_behind(): lax.ppermute(value, axis, [(source, source + steps) for source in range(l...  25.7 us
    ppermute x11, starting transfers between devices, from_behind(): lax.ppermute(value, axis, [(source, source + steps) for source in range(l...  24.5 us
    sub x5, other arithmetic, local(): smooth = source - lam * divergence(first, second)  24.3 us
    another operation x6, other arithmetic, mixing_matrix(): lax.linalg.triangular_solve(factor, image, left_side=False, lower=True, t...  16.6 us
    slice x5, local copies, waits for them, and re-layouts, col_grad(): next_cols = jnp.pad(smooth[:, :, :, 1:], ((0, 0), (0, 0), (0, 0), (0, 1)))  13.5 us
  transfers between devices with their start and end apart: 17, of which 10 were waited for; matrix products, arithmetic and copies ran while one was open for 25% of the time, Pallas kernels for 0%

profile of v1, /device:TPU:8, one launch (start us, length us, event | category | flops | bytes accessed | tf_op | source)
XLA Modules:
  0.0 344.2 jit_solution(17491802390838344083)
XLA Ops:
  7.3 1.5 convert_element_type.88
  9.7 3.6 %fusion = bf16[32,4,16,512]{3,0,2,1:T(8,128)(2,1)S(1)} fusion(bf16[32,4,16,512]{3,2,1,0:T(8,128)(2,1)S(1)} %copy-done.7, f32[32,16,512]{2,0,1:T(8,128)S(1)} %copy.22, pred[4]{0:T(512)(128)(4,1)S(1)} %iota_compare_fusion.3, bf16[32,4,16,512]{3,2,1,0:T(8,128)(2,1)S(1)} %copy-done.2), kind=kLoop, calls=%fused_computation.5 | loop fusion | flops 6291456 | bytes 7340036 | tf_op jit(solution)/shard_map/convert_element_type | solution.py:83
  13.3 1.5 copy.30
  14.9 85.5 %all-gather.2.cloned.1.call-done = bf16[128,32768]{1,0:T(8,128)(2,1)} async-done(((bf16[32,32768]{1,0:T(8,128)(2,1)}), bf16[128,32768]{1,0:T(8,128)(2,1)}) %all-gather.2.cloned.1.call-update) | async-done | bytes 8388624 | tf_op jit(solution)/shard_map/all_gather | solution.py:87
  100.3 6.9 %fusion.61 = f32[128,32]{0,1:T(8,128)S(1)} fusion(bf16[128,32768]{1,0:T(8,128)(2,1)} %all-gather.2.cloned.1.call-done, bf16[32,32768]{1,0:T(8,128)(2,1)} %bitcast.91), kind=kOutput, calls=%fused_computation.132 | convolution fusion | flops 268435456 | bytes 10502144 | tf_op jit(solution)/shard_map/dot_general | solution.py:49
  107.3 1.2 collective-permute-done
  108.4 1.6 collective-permute-start.1
  110.0 2.2 collective-permute-done.1
  112.2 3.1 collective-permute-start.2
  116.0 1.9 collective-permute-start.5
  118.0 3.7 %collective-permute-done.3 = f32[128,32]{0,1:T(8,128)S(1)} collective-permute-done((f32[128,32]{0,1:T(8,128)S(1)}, f32[128,32]{0,1:T(8,128)S(1)}, u32[]{:S(2)}, u32[]{:S(2)}) %collective-permute-start.3) | collective-permute-done | bytes 16416 | tf_op jit(solution)/shard_map/ppermute | solution.py:91
  121.8 2.1 collective-permute-start.4
  124.0 3.0 collective-permute-done.4
  127.0 12.1 %all_gather.7 = f32[128,128]{0,1:T(8,128)S(1)} all-gather(f32[128,32]{0,1:T(8,128)S(1)} %add.117), channel_id=1, replica_groups=mesh['frame'=4,'pix'=32] {'frame'}, dimensions={1}, use_global_device_ids=true | all-gather | bytes 81920 | tf_op jit(solution)/shard_map/all_gather | solution.py:92
  139.5 5.8 %cholesky.74 = f32[64,64]{1,0:T(8,128)S(1)} custom-call(f32[64,64]{1,0:T(8,128)S(1)} %add_multiply_fusion), custom_call_target="Cholesky" | custom-call | tf_op jit(solution)/shard_map/jit(cholesky)/cholesky | solution.py:33
  146.7 4.9 %custom-call.13 = f32[1,64,64]{1,2,0:T(8,128)S(1)} custom-call(f32[1,64,64]{2,1,0:T(8,128)S(1)} %fusion.32), custom_call_target="InvertDiagBlocksLowerTriangular" | custom-call | tf_op jit(solution)/shard_map/triangular_solve/custom-call.0 | solution.py:34
  152.4 5.8 %cholesky.85 = f32[64,64]{1,0:T(8,128)S(1)} custom-call(f32[64,64]{1,0:T(8,128)S(1)} %fusion.44), custom_call_target="Cholesky" | custom-call | tf_op jit(solution)/shard_map/jit(cholesky)/cholesky | solution.py:33
  159.5 4.9 %custom-call.14 = f32[1,64,64]{1,2,0:T(8,128)S(1)} custom-call(f32[1,64,64]{2,1,0:T(8,128)S(1)} %fusion.33), custom_call_target="InvertDiagBlocksLowerTriangular" | custom-call | tf_op jit(solution)/shard_map/triangular_solve/custom-call.0 | solution.py:34
  165.2 5.8 %cholesky.96 = f32[64,64]{1,0:T(8,128)S(1)} custom-call(f32[64,64]{1,0:T(8,128)S(1)} %fusion.42), custom_call_target="Cholesky" | custom-call | tf_op jit(solution)/shard_map/jit(cholesky)/cholesky | solution.py:33
  172.4 4.9 %custom-call.15 = f32[1,64,64]{1,2,0:T(8,128)S(1)} custom-call(f32[1,64,64]{2,1,0:T(8,128)S(1)} %fusion.34), custom_call_target="InvertDiagBlocksLowerTriangular" | custom-call | tf_op jit(solution)/shard_map/triangular_solve/custom-call.0 | solution.py:34
  178.2 5.8 %cholesky.107 = f32[64,64]{1,0:T(8,128)S(1)} custom-call(f32[64,64]{1,0:T(8,128)S(1)} %fusion.40), custom_call_target="Cholesky" | custom-call | tf_op jit(solution)/shard_map/jit(cholesky)/cholesky | solution.py:38
  185.4 4.9 %custom-call.10 = f32[1,64,64]{1,2,0:T(8,128)S(1)} custom-call(f32[1,64,64]{2,1,0:T(8,128)S(1)} %fusion.35), custom_call_target="InvertDiagBlocksLowerTriangular" | custom-call | tf_op jit(solution)/shard_map/triangular_solve | solution.py:42
  191.1 4.6 %convolution_convert_fusion = bf16[32,32768]{1,0:T(8,128)(2,1)S(1)} fusion(bf16[128,32768]{1,0:T(8,128)(2,1)} %all-gather.2.cloned.1.call-done, bf16[128,128]{0,1:T(8,128)(2,1)S(1)} %fusion.66, s32[]{:T(128)S(6)} %select_n.43), kind=kOutput, calls=%fused_computation | convolution fusion | flops 269484032 | bytes 10493956 | tf_op jit(solution)/shard_map/dot_general | solution.py:55
  195.7 0.7 copy.31
  196.4 3.5 %multiply_subtract_fusion = f32[32,4,16,512]{3,0,2,1:T(8,128)S(1)} fusion(f32[512]{0:T(512)S(1)} %pad_subtract_fusion, bf16[32,4,1,512]{3,0,2,1:T(8,128)(2,1)S(1)} %collective-permute-done.5, f32[4]{0:T(128)S(1)} %copy-done.8, f32[32,16,512]{2,0,1:T(8,128)S(1)} %copy.22, pred[4]{0:T(512)(128)(4,1)S(1)} %iota_compare_fusion.3, ...), kind=kLoop, calls=%fused_computation.57 | loop fusion | flops 10485760 | bytes 9570324 | tf_op jit(solution)/shard_map/sub | solution.py:114
  199.9 1.9 copy-done.5
  201.8 1.9 collective-permute-start.6
  203.8 2.2 copy-done.6
  206.0 1.1 slice.151
  207.1 0.9 slice-done
  208.1 3.6 %subtract_divide_fusion.8 = (f32[32,4,16,512]{3,0,2,1:T(8,128)S(1)}, f32[32,4,16,512]{3,0,2,1:T(8,128)S(1)}) fusion(f32[4]{0:T(128)S(1)} %broadcast_divide_fusion, f32[32,4,16,512]{3,0,2,1:T(8,128)S(1)} %copy-done.6, f32[32,4,16,511]{3,0,2,1:T(8,128)S(1)} %slice.151, pred[512]{0:T(512)(128)(4,1)S(1)} %iota_compare_fusion.2, ...), kind=kLoop, calls=%fused_computation.53 | loop fusion | flops 16777216 | bytes 20963872 | tf_op jit(solution)/shard_map/div | solution.py:63
  211.7 2.5 collective-permute-start.7
  214.3 0.7 slice.153
  215.0 5.3 %collective-permute-done.7 = bf16[32,4,1,512]{3,0,2,1:T(8,128)(2,1)S(1)} collective-permute-done((bf16[32,4,1,512]{3,0,2,1:T(8,128)(2,1)S(1)}, bf16[32,4,1,512]{3,0,2,1:T(8,128)(2,1)S(1)}, u32[]{:S(2)}, u32[]{:S(2)}) %collective-permute-start.7) | collective-permute-done | bytes 131104 | tf_op jit(solution)/shard_map/ppermute | solution.py:22
  220.3 5.2 %fusion.4 = f32[32,4,16,512]{3,0,2,1:T(8,128)S(1)} fusion(f32[32,4,16,512]{3,0,2,1:T(8,128)S(1)} %get-tuple-element.17, f32[32,4,15,512]{3,0,2,1:T(8,128)S(1)} %slice.153, f32[32,4,1,512]{3,0,2,1:T(8,128)S(1)} %convert_element_type.96, f32[32,4,16,512]{3,0,2,1:T(8,128)S(1)} %get-tuple-element.16, f32[32,4,16,511]{3,0,2,1:T(8,128)S(1)} %bitcast.88, ...), kind=kLoop, calls=%fused_computation.11 | loop fusion | flops 11534336 | bytes 26206228 | tf_op jit(solution)/shard_map/sub | solution.py:114
  225.5 1.9 collective-permute-start.8
  227.5 2.6 slice.155
  230.1 3.1 slice.157
  233.2 5.9 %subtract_divide_fusion.6 = (f32[32,4,16,512]{3,0,2,1:T(8,128)S(1)}, f32[32,4,16,512]{3,0,2,1:T(8,128)S(1)}) fusion(f32[32,4,16,512]{3,0,2,1:T(8,128)S(1)} %get-tuple-element.16, f32[4]{0:T(128)S(1)} %broadcast_divide_fusion, f32[32,4,16,512]{3,0,2,1:T(8,128)S(1)} %fusion.4, f32[32,4,16,511]{3,0,2,1:T(8,128)} %slice.157, ...), kind=kLoop, calls=%fused_computation.49 | loop fusion | flops 16777216 | bytes 29352480 | tf_op jit(solution)/shard_map/div | solution.py:63
  239.1 2.8 collective-permute-start.9
  242.7 4.8 %collective-permute-done.9 = bf16[32,4,1,512]{3,0,2,1:T(8,128)(2,1)S(1)} collective-permute-done((bf16[32,4,1,512]{3,0,2,1:T(8,128)(2,1)S(1)}, bf16[32,4,1,512]{3,0,2,1:T(8,128)(2,1)S(1)}, u32[]{:S(2)}, u32[]{:S(2)}) %collective-permute-start.9) | collective-permute-done | bytes 131104 | tf_op jit(solution)/shard_map/ppermute | solution.py:22
  247.6 5.2 %fusion.8 = f32[32,4,16,512]{3,0,2,1:T(8,128)S(1)} fusion(f32[32,4,16,512]{3,0,2,1:T(8,128)S(1)} %get-tuple-element.15, f32[32,4,15,512]{3,0,2,1:T(8,128)S(1)} %slice.159, f32[32,4,1,512]{3,0,2,1:T(8,128)S(1)} %convert_element_type.98, f32[32,4,16,512]{3,0,2,1:T(8,128)S(1)} %get-tuple-element.14, f32[32,4,16,511]{3,0,2,1:T(8,128)S(1)} %bitcast.86, ...), kind=kLoop, calls=%fused_computation.17 | loop fusion | flops 11534336 | bytes 26206228 | tf_op jit(solution)/shard_map/sub | solution.py:114
  252.8 1.9 collective-permute-start.10
  254.7 2.6 slice.161
  257.4 3.1 slice.163
  260.5 5.9 %subtract_divide_fusion.4 = (f32[32,4,16,512]{3,0,2,1:T(8,128)S(1)}, f32[32,4,16,512]{3,0,2,1:T(8,128)S(1)}) fusion(f32[32,4,16,512]{3,0,2,1:T(8,128)S(1)} %get-tuple-element.14, f32[4]{0:T(128)S(1)} %broadcast_divide_fusion, f32[32,4,16,512]{3,0,2,1:T(8,128)S(1)} %fusion.8, f32[32,4,16,511]{3,0,2,1:T(8,128)} %slice.163, ...), kind=kLoop, calls=%fused_computation.45 | loop fusion | flops 16777216 | bytes 29352480 | tf_op jit(solution)/shard_map/div | solution.py:63
  266.4 2.4 collective-permute-start.11
  269.5 5.3 %collective-permute-done.11 = bf16[32,4,1,512]{3,0,2,1:T(8,128)(2,1)S(1)} collective-permute-done((bf16[32,4,1,512]{3,0,2,1:T(8,128)(2,1)S(1)}, bf16[32,4,1,512]{3,0,2,1:T(8,128)(2,1)S(1)}, u32[]{:S(2)}, u32[]{:S(2)}) %collective-permute-start.11) | collective-permute-done | bytes 131104 | tf_op jit(solution)/shard_map/ppermute | solution.py:22
  274.8 5.2 %fusion.12 = f32[32,4,16,512]{3,0,2,1:T(8,128)S(1)} fusion(f32[32,4,16,512]{3,0,2,1:T(8,128)S(1)} %get-tuple-element.13, f32[32,4,15,512]{3,0,2,1:T(8,128)S(1)} %slice.165, f32[32,4,1,512]{3,0,2,1:T(8,128)S(1)} %convert_element_type.100, f32[32,4,16,512]{3,0,2,1:T(8,128)S(1)} %get-tuple-element.12, f32[32,4,16,511]{3,0,2,1:T(8,128)S(1)} %bitcast.87, ...), kind=kLoop, calls=%fused_computation.23 | loop fusion | flops 11534336 | bytes 26206228 | tf_op jit(solution)/shard_map/sub | solution.py:114
  280.1 2.1 collective-permute-start.12
  282.2 2.6 slice.167
  284.8 3.1 slice.169
  287.9 5.9 %subtract_divide_fusion.2 = (f32[32,4,16,512]{3,0,2,1:T(8,128)S(1)}, f32[32,4,16,512]{3,0,2,1:T(8,128)S(1)}) fusion(f32[32,4,16,512]{3,0,2,1:T(8,128)S(1)} %get-tuple-element.12, f32[4]{0:T(128)S(1)} %broadcast_divide_fusion, f32[32,4,16,512]{3,0,2,1:T(8,128)S(1)} %fusion.12, f32[32,4,16,511]{3,0,2,1:T(8,128)} %slice.169, ...), kind=kLoop, calls=%fused_computation.41 | loop fusion | flops 16777216 | bytes 29352480 | tf_op jit(solution)/shard_map/div | solution.py:63
  293.8 2.4 collective-permute-start.13
  297.0 5.3 %collective-permute-done.13 = bf16[32,4,1,512]{3,0,2,1:T(8,128)(2,1)S(1)} collective-permute-done((bf16[32,4,1,512]{3,0,2,1:T(8,128)(2,1)S(1)}, bf16[32,4,1,512]{3,0,2,1:T(8,128)(2,1)S(1)}, u32[]{:S(2)}, u32[]{:S(2)}) %collective-permute-start.13) | collective-permute-done | bytes 131104 | tf_op jit(solution)/shard_map/ppermute | solution.py:22
  302.3 5.2 %fusion.16 = f32[32,4,16,512]{3,0,2,1:T(8,128)S(1)} fusion(f32[32,4,16,512]{3,0,2,1:T(8,128)S(1)} %get-tuple-element.11, f32[32,4,15,512]{3,0,2,1:T(8,128)S(1)} %slice.171, f32[32,4,1,512]{3,0,2,1:T(8,128)S(1)} %convert_element_type.102, f32[32,4,16,512]{3,0,2,1:T(8,128)S(1)} %get-tuple-element.10, f32[32,4,16,511]{3,0,2,1:T(8,128)S(1)} %bitcast.85, ...), kind=kLoop, calls=%fused_computation.29 | loop fusion | flops 11534336 | bytes 26206228 | tf_op jit(solution)/shard_map/sub | solution.py:114
  307.5 1.9 collective-permute-start.14
  309.4 2.6 slice.173
  312.1 3.1 slice.175
  315.2 5.9 %subtract_divide_fusion = (f32[32,4,16,512]{3,0,2,1:T(8,128)S(1)}, f32[32,4,16,512]{3,0,2,1:T(8,128)S(1)}) fusion(f32[32,4,16,512]{3,0,2,1:T(8,128)S(1)} %get-tuple-element.10, f32[4]{0:T(128)S(1)} %broadcast_divide_fusion, f32[32,4,16,512]{3,0,2,1:T(8,128)S(1)} %fusion.16, f32[32,4,16,511]{3,0,2,1:T(8,128)} %slice.175, ...), kind=kLoop, calls=%fused_computation.37 | loop fusion | flops 16777216 | bytes 29352480 | tf_op jit(solution)/shard_map/div | solution.py:63
  321.1 2.6 collective-permute-start.15
  324.5 5.0 %collective-permute-done.15 = bf16[32,4,1,512]{3,0,2,1:T(8,128)(2,1)S(1)} collective-permute-done((bf16[32,4,1,512]{3,0,2,1:T(8,128)(2,1)S(1)}, bf16[32,4,1,512]{3,0,2,1:T(8,128)(2,1)S(1)}, u32[]{:S(2)}, u32[]{:S(2)}) %collective-permute-start.15) | collective-permute-done | bytes 131104 | tf_op jit(solution)/shard_map/ppermute | solution.py:22
  329.5 5.1 %fusion.21 = bf16[32,4,16,512]{3,0,2,1:T(8,128)(2,1)S(1)} fusion(f32[32,4,16,512]{3,0,2,1:T(8,128)S(1)} %get-tuple-element.9, f32[32,4,15,512]{3,0,2,1:T(8,128)S(1)} %slice.177, f32[32,4,1,512]{3,0,2,1:T(8,128)S(1)} %convert_element_type.104, f32[32,4,16,512]{3,0,2,1:T(8,128)S(1)} %get-tuple-element.8, f32[32,4,16,511]{3,0,2,1:T(8,128)S(1)} %bitcast.89, ...), kind=kLoop, calls=%fused_computation.36 | loop fusion | flops 12582912 | bytes 24109076 | tf_op jit(solution)/shard_map/convert_element_type | solution.py:121
  334.7 2.5 copy.29
  (100 shorter events, 14.1 us)
Async XLA Ops:
  7.2 131.9 %copy-start = (f32[128,64]{0,1:T(8,128)S(1)}, f32[128,64]{0,1:T(8,128)}, u32[]{:S(2)}) copy-start(f32[128,64]{0,1:T(8,128)} %param.11) | copy-start | bytes 98308
  7.2 2.2 copy-start.2
  7.2 93.1 %all-gather.2.cloned.1.call-start = ((), (), s32[]{:S(2)}) async-start(), calls=%async_computation | async-start | bytes 10485760 | tf_op jit(solution)/shard_map/all_gather | solution.py:87
  7.2 2.5 copy-start.7
  14.8 103.2 %copy-start.8 = (f32[4]{0:T(128)S(1)}, f32[4]{0:T(128)}, u32[]{:S(2)}) copy-start(f32[4]{0:T(128)} %param.12) | copy-start | bytes 52
  107.2 1.2 collective-permute-start
  108.4 3.7 %collective-permute-start.1 = (f32[128,32]{0,1:T(8,128)S(1)}, f32[128,32]{0,1:T(8,128)S(1)}, u32[]{:S(2)}, u32[]{:S(2)}) collective-permute-start(f32[128,32]{0,1:T(8,128)S(1)} %add.113), channel_id=1, source_target_pairs={{0,2},{1,3},{2,0},{3,1},{4,6},{5,7},{6,4},{7,5},{8,10},{9,11},{10,... | collective-permute-start | bytes 49160 | tf_op jit(solution)/shard_map/ppermute | solution.py:91
  112.2 5.7 %collective-permute-start.2 = (f32[128,32]{0,1:T(8,128)S(1)}, f32[128,32]{0,1:T(8,128)S(1)}, u32[]{:S(2)}, u32[]{:S(2)}) collective-permute-start(f32[128,32]{0,1:T(8,128)S(1)} %add.114), channel_id=1, source_target_pairs={{0,4},{1,5},{2,6},{3,7},{4,0},{5,1},{6,2},{7,3},{8,12},{9,13},{10,... | collective-permute-start | bytes 49160 | tf_op jit(solution)/shard_map/ppermute | solution.py:91
  116.0 80.4 %collective-permute-start.5 = (bf16[32,4,1,512]{3,0,2,1:T(8,128)(2,1)}, bf16[32,4,1,512]{3,0,2,1:T(8,128)(2,1)S(1)}, u32[]{:S(2)}, u32[]{:S(2)}) collective-permute-start(bf16[32,4,1,512]{3,0,2,1:T(8,128)(2,1)} %convert_element_type.94), channel_id=1, source_target_pairs={{0,1},{1,2},{2,3},{3,4},{4,5},{5,6},{6,7},{7,8},{8,9},{9,10},{10,1... | collective-permute-start | bytes 393224 | tf_op jit(solution)/shard_map/ppermute | solution.py:22
  117.9 3.8 %collective-permute-start.3 = (f32[128,32]{0,1:T(8,128)S(1)}, f32[128,32]{0,1:T(8,128)S(1)}, u32[]{:S(2)}, u32[]{:S(2)}) collective-permute-start(f32[128,32]{0,1:T(8,128)S(1)} %add.115), channel_id=1, source_target_pairs={{0,8},{1,9},{2,10},{3,11},{4,12},{5,13},{6,14},{7,15},{8,0},{9,1},... | collective-permute-start | bytes 49160 | tf_op jit(solution)/shard_map/ppermute | solution.py:91
  121.8 5.2 %collective-permute-start.4 = (f32[128,32]{0,1:T(8,128)S(1)}, f32[128,32]{0,1:T(8,128)S(1)}, u32[]{:S(2)}, u32[]{:S(2)}) collective-permute-start(f32[128,32]{0,1:T(8,128)S(1)} %add.116), channel_id=1, source_target_pairs={{0,16},{1,17},{2,18},{3,19},{4,20},{5,21},{6,22},{7,23},{8,24},{9,... | collective-permute-start | bytes 49160 | tf_op jit(solution)/shard_map/ppermute | solution.py:91
  196.4 3.5 %copy-start.3 = (bf16[4,8,64,512]{3,2,1,0:T(8,128)(2,1)}, bf16[4,8,64,512]{3,2,1,0:T(8,128)(2,1)S(1)}, u32[]{:S(2)}) copy-start(bf16[4,8,64,512]{3,2,1,0:T(8,128)(2,1)S(1)} %copy.31) | copy-start | bytes 6291460
  199.9 2.0 copy-start.5
  201.8 5.3 %collective-permute-start.6 = (bf16[32,4,1,512]{3,0,2,1:T(8,128)(2,1)S(1)}, bf16[32,4,1,512]{3,0,2,1:T(8,128)(2,1)S(1)}, u32[]{:S(2)}, u32[]{:S(2)}) collective-permute-start(bf16[32,4,1,512]{3,0,2,1:T(8,128)(2,1)S(1)} %slice.198), channel_id=1, source_target_pairs={{1,0},{2,1},{3,2},{4,3},{5,4},{6,5},{7,6},{8,7},{9,8},{10,9},{11,1... | collective-permute-start | bytes 393224 | tf_op jit(solution)/shard_map/ppermute | solution.py:22
  203.8 2.2 copy-start.6
  206.0 2.1 slice-start
  211.7 8.6 %copy-start.4 = (bf16[4,8,64,512]{3,2,1,0:T(8,128)(2,1)S(1)}, bf16[4,8,64,512]{3,2,1,0:T(8,128)(2,1)}, u32[]{:S(2)}) copy-start(bf16[4,8,64,512]{3,2,1,0:T(8,128)(2,1)} %copy-done.3) | copy-start | bytes 6291460
  211.7 8.5 %collective-permute-start.7 = (bf16[32,4,1,512]{3,0,2,1:T(8,128)(2,1)S(1)}, bf16[32,4,1,512]{3,0,2,1:T(8,128)(2,1)S(1)}, u32[]{:S(2)}, u32[]{:S(2)}) collective-permute-start(bf16[32,4,1,512]{3,0,2,1:T(8,128)(2,1)S(1)} %slice.197), channel_id=1, source_target_pairs={{0,1},{1,2},{2,3},{3,4},{4,5},{5,6},{6,7},{7,8},{8,9},{9,10},{10,1... | collective-permute-start | bytes 393224 | tf_op jit(solution)/shard_map/ppermute | solution.py:22
  225.5 7.7 %collective-permute-start.8 = (bf16[32,4,1,512]{3,0,2,1:T(8,128)(2,1)S(1)}, bf16[32,4,1,512]{3,0,2,1:T(8,128)(2,1)S(1)}, u32[]{:S(2)}, u32[]{:S(2)}) collective-permute-start(bf16[32,4,1,512]{3,0,2,1:T(8,128)(2,1)S(1)} %slice.196), channel_id=1, source_target_pairs={{1,0},{2,1},{3,2},{4,3},{5,4},{6,5},{7,6},{8,7},{9,8},{10,9},{11,1... | collective-permute-start | bytes 393224 | tf_op jit(solution)/shard_map/ppermute | solution.py:22
  239.1 8.4 %collective-permute-start.9 = (bf16[32,4,1,512]{3,0,2,1:T(8,128)(2,1)S(1)}, bf16[32,4,1,512]{3,0,2,1:T(8,128)(2,1)S(1)}, u32[]{:S(2)}, u32[]{:S(2)}) collective-permute-start(bf16[32,4,1,512]{3,0,2,1:T(8,128)(2,1)S(1)} %slice.195), channel_id=1, source_target_pairs={{0,1},{1,2},{2,3},{3,4},{4,5},{5,6},{6,7},{7,8},{8,9},{9,10},{10,1... | collective-permute-start | bytes 393224 | tf_op jit(solution)/shard_map/ppermute | solution.py:22
  252.8 7.7 %collective-permute-start.10 = (bf16[32,4,1,512]{3,0,2,1:T(8,128)(2,1)S(1)}, bf16[32,4,1,512]{3,0,2,1:T(8,128)(2,1)S(1)}, u32[]{:S(2)}, u32[]{:S(2)}) collective-permute-start(bf16[32,4,1,512]{3,0,2,1:T(8,128)(2,1)S(1)} %slice.194), channel_id=1, source_target_pairs={{1,0},{2,1},{3,2},{4,3},{5,4},{6,5},{7,6},{8,7},{9,8},{10,9},{11,1... | collective-permute-start | bytes 393224 | tf_op jit(solution)/shard_map/ppermute | solution.py:22
  266.4 8.4 %collective-permute-start.11 = (bf16[32,4,1,512]{3,0,2,1:T(8,128)(2,1)S(1)}, bf16[32,4,1,512]{3,0,2,1:T(8,128)(2,1)S(1)}, u32[]{:S(2)}, u32[]{:S(2)}) collective-permute-start(bf16[32,4,1,512]{3,0,2,1:T(8,128)(2,1)S(1)} %slice.193), channel_id=1, source_target_pairs={{0,1},{1,2},{2,3},{3,4},{4,5},{5,6},{6,7},{7,8},{8,9},{9,10},{10,1... | collective-permute-start | bytes 393224 | tf_op jit(solution)/shard_map/ppermute | solution.py:22
  280.1 7.8 %collective-permute-start.12 = (bf16[32,4,1,512]{3,0,2,1:T(8,128)(2,1)S(1)}, bf16[32,4,1,512]{3,0,2,1:T(8,128)(2,1)S(1)}, u32[]{:S(2)}, u32[]{:S(2)}) collective-permute-start(bf16[32,4,1,512]{3,0,2,1:T(8,128)(2,1)S(1)} %slice.192), channel_id=1, source_target_pairs={{1,0},{2,1},{3,2},{4,3},{5,4},{6,5},{7,6},{8,7},{9,8},{10,9},{11,1... | collective-permute-start | bytes 393224 | tf_op jit(solution)/shard_map/ppermute | solution.py:22
  293.8 8.4 %collective-permute-start.13 = (bf16[32,4,1,512]{3,0,2,1:T(8,128)(2,1)S(1)}, bf16[32,4,1,512]{3,0,2,1:T(8,128)(2,1)S(1)}, u32[]{:S(2)}, u32[]{:S(2)}) collective-permute-start(bf16[32,4,1,512]{3,0,2,1:T(8,128)(2,1)S(1)} %slice.191), channel_id=1, source_target_pairs={{0,1},{1,2},{2,3},{3,4},{4,5},{5,6},{6,7},{7,8},{8,9},{9,10},{10,1... | collective-permute-start | bytes 393224 | tf_op jit(solution)/shard_map/ppermute | solution.py:22
  307.5 7.7 %collective-permute-start.14 = (bf16[32,4,1,512]{3,0,2,1:T(8,128)(2,1)S(1)}, bf16[32,4,1,512]{3,0,2,1:T(8,128)(2,1)S(1)}, u32[]{:S(2)}, u32[]{:S(2)}) collective-permute-start(bf16[32,4,1,512]{3,0,2,1:T(8,128)(2,1)S(1)} %slice.190), channel_id=1, source_target_pairs={{1,0},{2,1},{3,2},{4,3},{5,4},{6,5},{7,6},{8,7},{9,8},{10,9},{11,1... | collective-permute-start | bytes 393224 | tf_op jit(solution)/shard_map/ppermute | solution.py:22
  321.1 8.4 %collective-permute-start.15 = (bf16[32,4,1,512]{3,0,2,1:T(8,128)(2,1)S(1)}, bf16[32,4,1,512]{3,0,2,1:T(8,128)(2,1)S(1)}, u32[]{:S(2)}, u32[]{:S(2)}) collective-permute-start(bf16[32,4,1,512]{3,0,2,1:T(8,128)(2,1)S(1)} %slice.189), channel_id=1, source_target_pairs={{0,1},{1,2},{2,3},{3,4},{4,5},{5,6},{6,7},{7,8},{8,9},{9,10},{10,1... | collective-permute-start | bytes 393224 | tf_op jit(solution)/shard_map/ppermute | solution.py:22
  329.5 7.6 %copy-start.1 = (f32[128,64]{0,1:T(8,128)S(1)}, f32[128,64]{0,1:T(8,128)}, u32[]{:S(2)}) copy-start(f32[128,64]{0,1:T(8,128)} %param.11) | copy-start | bytes 98308
Sparse Core Ops, SparseCore 0:
  15.0 85.3 all-gather.1
